TPU v7x, 32 devices: a whole 2x2x4 slice. The times are simulated.
32 devices in a mesh: mem: 8 (over z, y), lev: 4 (over x, core).
Axes of the slice: x: 2, y: 2, z: 4, core: 2. Of those that a mesh axis runs over, the one named last changes fastest.
Arguments:
- prior_ensemble_stack: float32 [16, 20, 64, 512], P('mem', 'lev'), may hold values from -6 to 6
- vertical_cfl_ratio: float32 [20, 64, 512], P('lev'), may hold values from -0.35 to 0.35
- horizontal_cfl_ratio: float32 [20, 64, 512], P('lev'), may hold values from -0.35 to 0.35
- spreading_coefficient: float32 [20], P('lev'), may hold values from 0.02 to 0.2
- obs_cells: int32 [2, 16], replicated, may hold values from 0 to 32767
- obs_slabs: int32 [2, 16], replicated, may hold values from 0 to 19
- obs_values: float32 [2, 16], replicated, may hold values from -6 to 6
- obs_error: float32 [2, 16], replicated, may hold values from 0.25 to 2
Outputs:
- analysis: float32 [16, 20, 64, 512], P('mem', 'lev')
All inputs are finite; a program needn't handle non-finite values.
Results may differ from a plain program's by a relative error of at most 0.0001.
Values sent between devices are 32-bit elements; how exact they have to be, the bound alone decides.
No kernel may reach another device: no remote copies, remote signals or barrier semaphores. Data moves between devices by JAX's collectives and lax.ppermute only.
A program may use at most 256 MiB of HBM per device.

v0:
```python
import functools

import jax
import jax.numpy as jnp
from jax import lax
from jax.experimental import pallas as pl
from jax.experimental.pallas import tpu as pltpu
from jax.sharding import PartitionSpec as P


STEPS = 2
LOC_HALF = 64
LANES = 128
GRANT = 24 * 1024 * 1024
TILE = 8
VMEM = pl.BlockSpec(memory_space=pltpu.VMEM)
SMEM = pl.BlockSpec(memory_space=pltpu.SMEM)


def cost(flops, nbytes):
    return pl.CostEstimate(flops=flops, bytes_accessed=nbytes, transcendentals=0)


def taper(row_gap, col_gap):
    scaled = jnp.sqrt(row_gap * row_gap + col_gap * col_gap) * (1.0 / LOC_HALF)
    inner = (
        ((-0.25 * scaled + 0.5) * scaled + 0.625) * scaled - 5.0 / 3.0
    ) * scaled * scaled + 1.0
    safe = jnp.maximum(scaled, 1.0)
    outer = (
        ((((scaled * (1.0 / 12.0) - 0.5) * scaled + 0.625) * scaled + 5.0 / 3.0) * scaled - 5.0)
        * scaled
        + 4.0
        - (2.0 / 3.0) / safe
    )
    return jnp.where(scaled <= 1.0, inner, jnp.where(scaled < 2.0, outer, 0.0))


def chunks_of(slab_dev):
    first = max(1, (2 * slab_dev) // 5)
    if slab_dev == 1:
        return ((0, 1, False),)
    return ((0, first, False), (first, slab_dev - first, True))


def row_col(cell, nx):
    if nx & (nx - 1):
        return cell // nx, cell % nx
    return lax.shift_right_logical(cell, nx.bit_length() - 1), cell & (nx - 1)


def place(ref, k):
    return ref[k // ref.shape[1], k % ref.shape[1]]


def params():
    return pltpu.CompilerParams(vmem_limit_bytes=GRANT)


def blocks_in(refs, n, whole):
    me = lax.axis_index("mem")
    return [(refs[0].at[me ^ j] if whole else refs[j], me ^ j) for j in range(n)]


def block_shapes(n, whole, rows):
    if whole:
        return [jax.ShapeDtypeStruct((n, rows, LANES), jnp.float32)]
    return [jax.ShapeDtypeStruct((rows, LANES), jnp.float32)] * n


def forecast_kernel(parts, n, cells_hbm, slabs_hbm, spread_hbm, x_hbm, cv_hbm, ch_hbm, *rest):
    outs, arrays = [], []
    for start, count, whole in parts:
        width = 1 if whole else n
        arrays.append(rest[:width])
        outs.append(blocks_in(rest[:width], n, whole))
        rest = rest[width:]
    x_buf, cv_buf, ch_buf, cells, slabs, spread, spots, field, half, weights, picks = rest[:-2]
    sem, small = rest[-2:]
    mem_dev, slab_dev, tiles = x_buf.shape[:3]
    ny, nx = x_buf.shape[3] - 2 * TILE, tiles * LANES
    block = ny // n
    depth = block * tiles
    total = cells.shape[0] * cells.shape[1]

    def loads(c):
        slabs_of = slice(parts[c][0], parts[c][0] + parts[c][1])
        return [
            pltpu.make_async_copy(cv_hbm.at[slabs_of], cv_buf.at[slabs_of], sem.at[tiles, c]),
            pltpu.make_async_copy(ch_hbm.at[slabs_of], ch_buf.at[slabs_of], sem.at[tiles + 1, c]),
        ] + [
            pltpu.make_async_copy(
                x_hbm.at[:, slabs_of, :, t * LANES : (t + 1) * LANES],
                x_buf.at[:, slabs_of, t, TILE : TILE + ny, :],
                sem.at[t, c],
            )
            for t in range(tiles)
        ]

    lists = (
        pltpu.make_async_copy(spread_hbm, spread, small.at[0]),
        pltpu.make_async_copy(cells_hbm, cells, small.at[1]),
        pltpu.make_async_copy(slabs_hbm, slabs, small.at[2]),
    )
    for copy in [*loads(0), *lists] + [copy for c in range(1, len(parts)) for copy in loads(c)]:
        copy.start()
    for copy in lists:
        copy.wait()
    for k in range(total):
        row, col = row_col(place(cells, k), nx)
        across, wanted = row_col(col, LANES)
        off = place(slabs, k) - lax.axis_index("lev") * slab_dev
        inside = (off >= 0) & (off < slab_dev)
        spots[0, k] = jnp.where(inside, off, 0) * mem_dev
        spots[1, k] = across * ny + row
        spots[2, k] = jnp.where(inside, wanted, LANES)
    sub = lax.broadcasted_iota(jnp.int32, (TILE, LANES), 0)
    lane = lax.broadcasted_iota(jnp.int32, (TILE, LANES), 1)
    east_edge, west_edge = lane == LANES - 1, lane == 0
    high = ny // TILE

    def spot(r, t):
        return slice(t * ny + r * TILE, t * ny + (r + 1) * TILE)

    def advance(turn, load, keep, store):
        for r in range(high):
            row = TILE + r * TILE
            ahead, behind = {}, {}
            for m in range(mem_dev):
                for t in range(tiles):
                    f = load(m, t, row)
                    ahead[m, t] = pltpu.roll(f, LANES - 1, 1)
                    behind[m, t] = pltpu.roll(f, 1, 1)
            for t in range(tiles):
                at = spot(r, t)
                east_w, west_w = weights[turn, 0, at, :], weights[turn, 1, at, :]
                north_w, south_w = weights[turn, 2, at, :], weights[turn, 3, at, :]
                for m in range(mem_dev):
                    f = load(m, t, row)
                    east = jnp.where(east_edge, ahead.get((m, t + 1), f), ahead[m, t])
                    west = jnp.where(west_edge, behind.get((m, t - 1), f), behind[m, t])
                    if r + 1 < high:
                        north = load(m, t, row + 1)
                    else:
                        north = jnp.where(sub == TILE - 1, f, pltpu.roll(f, TILE - 1, 0))
                    if r > 0:
                        south = load(m, t, row - 1)
                    else:
                        south = jnp.where(sub == 0, f, pltpu.roll(f, 1, 0))
                    store(
                        m,
                        r,
                        t,
                        (keep * f + east_w * east)
                        + (west_w * west + north_w * north)
                        + south_w * south,
                    )

    for c, ((start, count, whole), blocks) in enumerate(zip(parts, outs)):
        direct = whole and block % TILE == 0
        for copy in loads(c):
            copy.wait()
        for s in range(count):
            slab = start + s
            diffuse = spread[slab]
            keep = 1.0 - 4.0 * diffuse
            for r in range(high):
                for t in range(tiles):
                    tile = (slice(r * TILE, (r + 1) * TILE), slice(t * LANES, (t + 1) * LANES))
                    half_v, half_h = 0.5 * cv_buf[slab, *tile], 0.5 * ch_buf[slab, *tile]
                    weights[s % 2, 0, spot(r, t), :] = diffuse - half_v
                    weights[s % 2, 1, spot(r, t), :] = diffuse + half_v
                    weights[s % 2, 2, spot(r, t), :] = diffuse - half_h
                    weights[s % 2, 3, spot(r, t), :] = diffuse + half_h

            def first(m, t, row):
                return x_buf[m, slab, t, row : row + TILE, :]

            def later(m, t, row):
                return half[s % 2 * mem_dev + m, t, row : row + TILE, :]

            def between(m, r, t, value):
                row = TILE + r * TILE
                half[s % 2 * mem_dev + m, t, row : row + TILE, :] = value

            def final(m, r, t, value):
                field[slab * mem_dev + m, spot(r, t), :] = value
                if direct:
                    at = (m * count + s) * depth + t * block + r * TILE % block
                    arrays[c][0][r * TILE // block, at : at + TILE, :] = value

            for step in range(STEPS):
                load, store = later if step else first, between if step < STEPS - 1 else final
                advance(s % 2, load, keep, store)

        def send(i, carry):
            level = start * mem_dev + i
            at = pl.multiple_of((i % mem_dev * count + i // mem_dev) * depth, TILE)
            for ref, d in blocks:
                for t in range(tiles):
                    row = pl.multiple_of(t * ny + d * block, block)
                    ref[pl.ds(at + t * block, block), :] = field[level, pl.ds(row, block), :]
            return carry

        if not direct:
            lax.fori_loop(0, count * mem_dev, send, 0)

    line_lane = lax.broadcasted_iota(jnp.int32, (1, LANES), 1)
    for k in range(total):
        level, row, wanted = spots[0, k], spots[1, k], spots[2, k]
        for m in range(mem_dev):
            line = field[level + m, pl.ds(row, 1), :]
            picks[m, pl.ds(k, 1), :] = jnp.where(line_lane == wanted, line, 0.0)
    diagonal = lax.broadcasted_iota(jnp.int32, (total, LANES), 0) == lax.broadcasted_iota(
        jnp.int32, (total, LANES), 1
    )
    values = []
    for m in range(mem_dev):
        value = jnp.sum(picks[m], axis=1, keepdims=True)
        values.append(jnp.sum(jnp.where(diagonal, value, 0.0), axis=0, keepdims=True))
    for j in range(n):
        seen = jnp.zeros((TILE, LANES), jnp.float32)
        for m in range(mem_dev):
            seen = jnp.where(sub == (j * mem_dev + m) % TILE, values[m], seen)
        outs[0][j][0][pl.ds(mem_dev * parts[0][1] * depth, TILE), :] = seen


def forecast(parts, n, cells, slabs, spread, x, cv, ch):
    mem_dev, slab_dev, ny, nx = x.shape
    depth = ny // n * nx // LANES
    shapes = []
    for i, (_, count, whole) in enumerate(parts):
        shapes.append(block_shapes(n, whole, mem_dev * count * depth + (0 if i else TILE)))
    outs = pl.pallas_call(
        functools.partial(forecast_kernel, parts, n),
        in_specs=[pl.BlockSpec(memory_space=pltpu.HBM)] * 6,
        out_specs=[VMEM for group in shapes for _ in group],
        out_shape=[shape for group in shapes for shape in group],
        scratch_shapes=[
            pltpu.VMEM((mem_dev, slab_dev, nx // LANES, ny + 2 * TILE, LANES), jnp.float32),
            pltpu.VMEM(cv.shape, jnp.float32),
            pltpu.VMEM(ch.shape, jnp.float32),
            pltpu.SMEM(cells.shape, jnp.int32),
            pltpu.SMEM(slabs.shape, jnp.int32),
            pltpu.SMEM(spread.shape, jnp.float32),
            pltpu.SMEM((3, cells.size), jnp.int32),
            pltpu.VMEM((slab_dev * mem_dev, ny * nx // LANES, LANES), jnp.float32),
            pltpu.VMEM((2 * mem_dev, nx // LANES, ny + 2 * TILE, LANES), jnp.float32),
            pltpu.VMEM((2, 4, ny * nx // LANES, LANES), jnp.float32),
            pltpu.VMEM((mem_dev, cells.size, LANES), jnp.float32),
            pltpu.SemaphoreType.DMA((2 + nx // LANES, len(parts))),
            pltpu.SemaphoreType.DMA((3,)),
        ],
        cost_estimate=cost(60 * x.size, 4 * (2 * x.size + 2 * cv.size)),
        compiler_params=params(),
        name="forecast",
    )(*[pltpu.with_memory_space_constraint(a, pltpu.HBM) for a in (cells, slabs, spread, x, cv, ch)])
    sends = []
    for group in shapes:
        sends.append(list(outs[: len(group)]))
        outs = outs[len(group) :]
    return sends


def reach(cells, lists, nx, block, groups):
    total = cells.shape[0] * cells.shape[1]
    me = lax.axis_index("mem")
    for g in range(groups):
        count = jnp.int32(0)
        low_col = g * TILE // block * LANES
        high_col = (g * TILE + TILE - 1) // block * LANES + LANES - 1
        low_row = me * block + g * TILE % block
        high_row = low_row + min(block, TILE) - 1
        for k in range(total):
            row, col = row_col(place(cells, k), nx)
            down = jnp.maximum(jnp.maximum(low_row - row, row - high_row), 0)
            across = jnp.maximum(jnp.maximum(low_col - col, col - high_col), 0)
            lists[g, count] = jnp.int32(k)
            near = down * down + across * across < (2 * LOC_HALF) ** 2
            count = count + near.astype(jnp.int32)
        lists[g, count] = jnp.int32(total)
        lists[g, total + 1] = count


def taper_kernel(nx, block, cells, values_ref, errors_ref, loc_ref, near_ref, meta_ref, out, lists, sem):
    total = near_ref.shape[0]
    depth = loc_ref.shape[1]
    at = lax.broadcasted_iota(jnp.int32, (depth, LANES), 0)
    cell_row = (lax.axis_index("mem") * block + at % block).astype(jnp.float32)
    cell_col = (
        at // block * LANES + lax.broadcasted_iota(jnp.int32, (depth, LANES), 1)
    ).astype(jnp.float32)
    lane = lax.broadcasted_iota(jnp.int32, (1, LANES), 1)
    row_of = jnp.zeros((1, LANES), jnp.float32)
    col_of = jnp.zeros((1, LANES), jnp.float32)
    for k in range(total):
        row, col = row_col(place(cells, k), nx)
        row, col = row.astype(jnp.float32), col.astype(jnp.float32)
        row_of = jnp.where(lane == k, row, row_of)
        col_of = jnp.where(lane == k, col, col_of)
        loc_ref[k] = taper(cell_row - row, cell_col - col)
        meta_ref[k, 0:1, :] = jnp.full((1, LANES), place(errors_ref, k), jnp.float32)
        meta_ref[k, 1:2, :] = jnp.full((1, LANES), place(values_ref, k), jnp.float32)
    loc_ref[total] = jnp.zeros((depth, LANES), jnp.float32)
    reach(cells, lists, nx, block, depth // TILE)
    copy = pltpu.make_async_copy(lists, out, sem)
    copy.start()
    diagonal = lax.broadcasted_iota(jnp.int32, (total, LANES), 0) == lax.broadcasted_iota(
        jnp.int32, (total, LANES), 1
    )
    own_row = jnp.sum(jnp.where(diagonal, row_of, 0.0), axis=1, keepdims=True)
    own_col = jnp.sum(jnp.where(diagonal, col_of, 0.0), axis=1, keepdims=True)
    near_ref[...] = taper(row_of - own_row, col_of - own_col)
    copy.wait()


def list_shape(depth):
    return (-(-depth // TILE // TILE) * TILE, LANES)


def taper_tables(nx, block, cells, values, errors):
    total = cells.size
    depth = block * nx // LANES
    return pl.pallas_call(
        functools.partial(taper_kernel, nx, block),
        in_specs=[SMEM] * 3,
        out_specs=[VMEM] * 4,
        out_shape=[
            jax.ShapeDtypeStruct((total + 1, depth, LANES), jnp.float32),
            jax.ShapeDtypeStruct((total, LANES), jnp.float32),
            jax.ShapeDtypeStruct((total, TILE, LANES), jnp.float32),
            jax.ShapeDtypeStruct(list_shape(depth), jnp.int32),
        ],
        scratch_shapes=[pltpu.SMEM(list_shape(depth), jnp.int32), pltpu.SemaphoreType.DMA(())],
        cost_estimate=cost(60 * total * depth * LANES, 4 * total * depth * LANES),
        compiler_params=params(),
        name="taper_tables",
    )(cells, values, errors)


def settle_blocks(n, mem_dev, count, depth, lists, anom_ref, incr_ref, loc_ref, ins, outs):
    total = loc_ref.shape[0] - 1
    members = n * mem_dev
    group = max(g for g in range(1, count + 1) if count % g == 0 and (g == 1 or g * members <= 48))
    turns = count // group

    def spread(ref, k, m):
        return ref[k, pl.ds(m, TILE, stride=0), :]

    def part(i, carry):
        tile, slab = i // turns, i % turns * group
        at = tile * TILE

        def spot(m, g):
            row = ((m % mem_dev) * count + slab + g) * depth + at
            return m // mem_dev, pl.ds(pl.multiple_of(row, TILE), TILE)

        xs = []
        for m in range(members):
            for g in range(group):
                src, row = spot(m, g)
                xs.append(ins[src][0][row, :])

        def step(k, xs):
            terms = [[] for _ in range(group)]
            for m in range(members):
                a = spread(anom_ref, k, m)
                for g in range(group):
                    terms[g].append(a * xs[m * group + g])
            loc = loc_ref[k, pl.ds(pl.multiple_of(at, TILE), TILE), :]
            for g in range(group):
                while len(terms[g]) > 1:
                    odd = terms[g][len(terms[g]) // 2 * 2 :]
                    terms[g] = [a + b for a, b in zip(terms[g][::2], terms[g][1::2])] + odd
            sums = [terms[g][0] * loc for g in range(group)]
            new = []
            for m in range(members):
                b = spread(incr_ref, k, m)
                for g in range(group):
                    new.append(xs[m * group + g] + b * sums[g])
            return new

        def two(i, xs):
            return tuple(step(lists[tile, 2 * i + 1], step(lists[tile, 2 * i], list(xs))))

        xs = lax.fori_loop(
            0, lax.shift_right_logical(lists[tile, total + 1] + 1, 1), two, tuple(xs)
        )
        for m in range(members):
            for g in range(group):
                src, row = spot(m, g)
                outs[src][0][row, :] = xs[m * group + g]
        return carry

    lax.fori_loop(0, depth // TILE * turns, part, 0)


def plan_kernel(n, mem_dev, count, lev, loc_ref, near_ref, meta_ref, lists_ref, *refs):
    seen_refs, refs = refs[:lev], refs[lev:]
    ins, refs = blocks_in(refs[:n], n, False), refs[n:]
    anom_ref, incr_ref = refs[:2]
    outs = blocks_in(refs[2 : 2 + n], n, False)
    lists, sem = refs[2 + n :]
    copy = pltpu.make_async_copy(lists_ref, lists, sem)
    copy.start()
    total, depth = near_ref.shape[0], loc_ref.shape[1]
    rows = seen_refs[0][...]
    for other in seen_refs[1:]:
        rows = rows + other[...]
    members = rows.shape[0]
    mean = jnp.sum(rows, axis=0, keepdims=True) * (1.0 / members)
    rows = rows - mean
    for k in range(total):
        error, value = meta_ref[k, 0:1, :], meta_ref[k, 1:2, :]
        anomaly = jnp.broadcast_to(rows[:, k : k + 1], rows.shape)
        ybar = jnp.broadcast_to(mean[:, k : k + 1], mean.shape)
        variance = jnp.sum(anomaly * anomaly, axis=0, keepdims=True) / (members - 1) + 1e-06
        shared = jnp.sum(rows * anomaly, axis=0, keepdims=True)
        scale = 1.0 / ((members - 1) * variance)
        shift = (ybar * error + value * variance) / (variance + error) - ybar
        shrink = jnp.sqrt(error / (variance + error)) - 1.0
        anom_ref[k, 0:members, :] = anomaly * scale
        incr_ref[k, 0:members, :] = shift + shrink * anomaly
        weight = near_ref[k : k + 1, :] * shared * scale
        mean = mean + weight * shift
        rows = rows + (weight * shrink) * anomaly
    anom_ref[total] = jnp.zeros(anom_ref.shape[1:], jnp.float32)
    incr_ref[total] = jnp.zeros(incr_ref.shape[1:], jnp.float32)
    copy.wait()
    settle_blocks(n, mem_dev, count, depth, lists, anom_ref, incr_ref, loc_ref, ins, outs)


def filter_plan(mem_dev, count, places, seen, xs):
    members = seen[0].shape[0]
    n = len(xs)
    total, depth = places[1].shape[0], places[0].shape[1]
    table = jax.ShapeDtypeStruct((total + 1, members + TILE, LANES), jnp.float32)
    shapes = [table, table] + block_shapes(n, False, mem_dev * count * depth)
    got = pl.pallas_call(
        functools.partial(plan_kernel, n, mem_dev, count, len(seen)),
        in_specs=[VMEM] * (4 + len(seen) + n),
        out_specs=[VMEM] * len(shapes),
        out_shape=shapes,
        scratch_shapes=[pltpu.SMEM(list_shape(depth), jnp.int32), pltpu.SemaphoreType.DMA(())],
        cost_estimate=cost(20_000_000, 4 * total * (2 * members + depth) * LANES),
        compiler_params=params(),
        name="filter_plan",
    )(*places, *seen, *xs)
    return got[:2], list(got[2:])


def settle_kernel(n, mem_dev, count, depth, whole, lists_ref, anom, incr, loc, *refs):
    width = 1 if whole else n
    ins, outs = blocks_in(refs[:width], n, whole), blocks_in(refs[width:-2], n, False)
    lists, sem = refs[-2:]
    copy = pltpu.make_async_copy(lists_ref, lists, sem)
    copy.start()
    copy.wait()
    settle_blocks(n, mem_dev, count, depth, lists, anom, incr, loc, ins, outs)


def settle(n, mem_dev, count, whole, places, tables, xs):
    loc, lists = places[0], places[3]
    depth = loc.shape[1]
    shapes = block_shapes(n, False, mem_dev * count * depth)
    size = n * mem_dev * count * depth * LANES
    return pl.pallas_call(
        functools.partial(settle_kernel, n, mem_dev, count, depth, whole),
        in_specs=[VMEM] * (4 + len(xs)),
        out_specs=[VMEM] * len(shapes),
        out_shape=shapes,
        scratch_shapes=[pltpu.SMEM(list_shape(depth), jnp.int32), pltpu.SemaphoreType.DMA(())],
        cost_estimate=cost(4 * loc.shape[0] * size, 8 * size),
        compiler_params=params(),
        name="settle",
    )(lists, *tables, loc, *xs)


def assemble_kernel(n, start, count, *refs):
    out_ref, stage, turn, sem = refs[-4:]
    blocks = blocks_in(refs[:n], n, False)
    mem_dev, _, ny, nx = out_ref.shape
    block = ny // n
    tiles = nx // LANES
    depth = block * tiles
    copies = []
    for slab in range(count):
        for m in range(mem_dev):
            at = (m * count + slab) * depth
            for t in range(tiles):
                lanes = slice(t * LANES, (t + 1) * LANES)
                lines = slice(at + t * block, at + (t + 1) * block)
                for j, (ref, d) in enumerate(blocks):
                    if block % TILE == 0:
                        row = pl.multiple_of(d * block, block)
                        stage[m, slab, pl.ds(row, block), lanes] = ref[lines, :]
                    else:
                        turn[j * block : (j + 1) * block, :] = ref[lines, :]
                if block % TILE:
                    for d, (_, j) in enumerate(blocks):
                        stage[m, slab, d * block : (d + 1) * block, lanes] = turn[
                            pl.ds(j * block, block), :
                        ]
        copies.append(
            pltpu.make_async_copy(
                stage.at[:, slab], out_ref.at[:, start + slab], sem.at[slab]
            )
        )
        copies[-1].start()
    for copy in copies:
        copy.wait()


def assemble(n, start, count, recv, shape, before):
    mem_dev, _, ny, nx = shape
    extra = [] if before is None else [before]
    return pl.pallas_call(
        functools.partial(assemble_kernel, n, start, count),
        in_specs=[VMEM] * n + [pl.BlockSpec(memory_space=pl.ANY)] * len(extra),
        out_specs=pl.BlockSpec(memory_space=pl.ANY),
        out_shape=jax.ShapeDtypeStruct(shape, jnp.float32),
        scratch_shapes=[
            pltpu.VMEM((mem_dev, count, ny, nx), jnp.float32),
            pltpu.VMEM((ny, LANES), jnp.float32),
            pltpu.SemaphoreType.DMA((count,)),
        ],
        input_output_aliases={} if before is None else {n: 0},
        cost_estimate=cost(0, 8 * n * recv[0].size),
        compiler_params=params(),
        name="assemble",
    )(*recv, *extra)


def order_of(n, first):
    far, near = list(range(n // 2, n)), list(range(2, n // 2)) + [1]
    if first == "far":
        return far + near
    if first == "near":
        return near + far
    return [j for pair in zip(far, near) for j in pair] + far[len(near) :]


def exchange(blocks, n, whole, first):
    if whole:
        return [lax.all_to_all(blocks[0], "mem", split_axis=0, concat_axis=0, tiled=True)]
    got = {}
    for j in order_of(n, first):
        got[j] = lax.ppermute(blocks[j], "mem", [(i, i ^ j) for i in range(n)])
    return blocks[:1] + [got[j] for j in range(1, n)]


def body(x, cv, ch, spread, obs_cells, obs_slabs, obs_values, obs_error):
    mem_dev, slab_dev, ny, nx = x.shape
    n, lev = lax.axis_size("mem"), lax.axis_size("lev")
    block = ny // n
    depth = block * nx // LANES
    parts = chunks_of(slab_dev)
    sends = forecast(parts, n, obs_cells, obs_slabs, spread, x, cv, ch)
    states = []
    for c, blocks in enumerate(sends):
        states.append(exchange(blocks, n, parts[c][2], "far"))
    per = TILE // mem_dev
    seen = [s[mem_dev * parts[0][1] * depth :, :] for s in states[0]]
    seen = jnp.concatenate([sum(seen[g : g + per]) for g in range(0, n, per)])
    tiles = [seen] + [
        lax.ppermute(seen, "lev", [(i, (i + d) % lev) for i in range(lev)])
        for d in range(1, lev)
    ]
    places = taper_tables(nx, block, obs_cells, obs_values, obs_error)
    result = None
    for c, ((start, count, whole), state) in enumerate(zip(parts, states)):
        if c == 0:
            tables, new = filter_plan(mem_dev, count, places, tiles, state)
        else:
            new = settle(n, mem_dev, count, whole, places, tables, state)
        back = exchange(list(new), n, False, "near" if c == 0 else "turns")
        result = assemble(n, start, count, back, x.shape, result)
    return result


def solution(mesh):
    in_specs = (
        P("mem", "lev", None, None),
        P("lev", None, None),
        P("lev", None, None),
        P("lev"),
        P(),
        P(),
        P(),
        P(),
    )
    out_specs = P("mem", "lev", None, None)
    return jax.shard_map(body, mesh=mesh, in_specs=in_specs, out_specs=out_specs, check_vma=False)
```

profile of v0, /device:TPU:0, one launch (start us, length us, event | category | flops | bytes accessed | tf_op | source)
XLA Modules:
  0.0 91.7 jit_solution(407807172491142196)
XLA Ops:
  0.0 3.9 %forecast.1 = (f32[136,128]{1,0:T(8,128)S(1)}, f32[136,128]{1,0:T(8,128)S(1)}, f32[136,128]{1,0:T(8,128)S(1)}, f32[136,128]{1,0:T(8,128)S(1)}, f32[136,128]{1,0:...) custom-call(s32[2,16]{1,0:T(2,128)} %cells_hbm.1, ...), custom_call_target="tpu_custom_call" | custom-call | flops 19660800 | bytes 3932160 | tf_op jit(solution)/shard_map/forecast/pallas_call | solution.py:234
  4.0 7.5 %all-to-all-start = ((f32[8,192,128]{2,1,0:T(8,128)}), f32[8,192,128]{2,1,0:T(8,128)S(1)}, u32[]{:S(2)}, u32[]{:S(2)}) async-start(f32[8,192,128]{2,1,0:T(8,128)} %get-tuple-element.50), calls=%async_computation | async-start | bytes 1572864 | tf_op jit(solution)/shard_map/all_to_all | solution.py:545
  11.4 2.0 %collective-permute-start = (f32[136,128]{1,0:T(8,128)S(1)}, f32[136,128]{1,0:T(8,128)S(1)}, u32[]{:S(2)}, u32[]{:S(2)}) collective-permute-start(f32[136,128]{1,0:T(8,128)S(1)} %get-tuple-element.41), channel_id=1, source_target_pairs={{0,4},{4,0},{8,12},{12,8},{16,20},{20,16},{24,28},{28,24},{1,5},{5... | collective-permute-start | bytes 208904 | tf_op jit(solution)/shard_map/ppermute | solution.py:548
  13.5 1.5 %collective-permute-start.1 = (f32[136,128]{1,0:T(8,128)S(1)}, f32[136,128]{1,0:T(8,128)S(1)}, u32[]{:S(2)}, u32[]{:S(2)}) collective-permute-start(f32[136,128]{1,0:T(8,128)S(1)} %get-tuple-element.42), channel_id=1, source_target_pairs={{0,8},{4,12},{8,0},{12,4},{16,24},{20,28},{24,16},{28,20},{1,9},{5... | collective-permute-start | bytes 208904 | tf_op jit(solution)/shard_map/ppermute | solution.py:548
  14.9 2.9 %collective-permute-start.3 = (f32[136,128]{1,0:T(8,128)S(1)}, f32[136,128]{1,0:T(8,128)S(1)}, u32[]{:S(2)}, u32[]{:S(2)}) collective-permute-start(f32[136,128]{1,0:T(8,128)S(1)} %get-tuple-element.44), channel_id=1, source_target_pairs={{0,16},{4,20},{8,24},{12,28},{16,0},{20,4},{24,8},{28,12},{1,17},{... | collective-permute-start | bytes 208904 | tf_op jit(solution)/shard_map/ppermute | solution.py:548
  20.3 2.4 %collective-permute-start.5 = (f32[136,128]{1,0:T(8,128)S(1)}, f32[136,128]{1,0:T(8,128)S(1)}, u32[]{:S(2)}, u32[]{:S(2)}) collective-permute-start(f32[136,128]{1,0:T(8,128)S(1)} %get-tuple-element.46), channel_id=1, source_target_pairs={{0,24},{4,28},{8,16},{12,20},{16,8},{20,12},{24,0},{28,4},{1,25},{... | collective-permute-start | bytes 208904 | tf_op jit(solution)/shard_map/ppermute | solution.py:548
  22.7 4.2 %collective-permute-done.1.refs_6_ = f32[136,128]{1,0:T(8,128)S(1)} collective-permute-done((f32[136,128]{1,0:T(8,128)S(1)}, f32[136,128]{1,0:T(8,128)S(1)}, u32[]{:S(2)}, u32[]{:S(2)}) %collective-permute-start.1) | collective-permute-done | bytes 69664 | tf_op jit(solution)/shard_map/ppermute | solution.py:548
  26.8 4.7 %collective-permute-start.6 = (f32[136,128]{1,0:T(8,128)S(1)}, f32[136,128]{1,0:T(8,128)S(1)}, u32[]{:S(2)}, u32[]{:S(2)}) collective-permute-start(f32[136,128]{1,0:T(8,128)S(1)} %get-tuple-element.47), channel_id=1, source_target_pairs={{0,28},{4,24},{8,20},{12,16},{16,12},{20,8},{24,4},{28,0},{1,29},{... | collective-permute-start | bytes 208904 | tf_op jit(solution)/shard_map/ppermute | solution.py:548
  31.6 8.8 %collective-permute-done.3.refs_8_ = f32[136,128]{1,0:T(8,128)S(1)} collective-permute-done((f32[136,128]{1,0:T(8,128)S(1)}, f32[136,128]{1,0:T(8,128)S(1)}, u32[]{:S(2)}, u32[]{:S(2)}) %collective-permute-start.3) | collective-permute-done | bytes 69664 | tf_op jit(solution)/shard_map/ppermute | solution.py:548
  40.4 2.0 %collective-permute-done.4.refs_9_ = f32[136,128]{1,0:T(8,128)S(1)} collective-permute-done((f32[136,128]{1,0:T(8,128)S(1)}, f32[136,128]{1,0:T(8,128)S(1)}, u32[]{:S(2)}, u32[]{:S(2)}) %collective-permute-start.4) | collective-permute-done | bytes 69664 | tf_op jit(solution)/shard_map/ppermute | solution.py:548
  42.5 1.6 %collective-permute-start.8 = (f32[16,128]{1,0:T(8,128)S(1)}, f32[16,128]{1,0:T(8,128)S(1)}, u32[]{:S(2)}, u32[]{:S(2)}) collective-permute-start(f32[16,128]{1,0:T(8,128)S(1)} %pad_maximum_fusion.refs_0_), channel_id=1, source_target_pairs={{0,2},{1,3},{2,0},{3,1},{4,6},{5,7},{6,4},{7,5},{8,10},{9,11},{10,... | collective-permute-start | bytes 24584 | tf_op jit(solution)/shard_map/ppermute | solution.py:566
  44.2 2.8 %taper_tables.1 = (f32[33,32,128]{2,1,0:T(8,128)S(1)}, f32[32,128]{1,0:T(8,128)S(1)}, f32[32,8,128]{2,1,0:T(8,128)S(1)}, s32[8,128]{1,0:T(8,128)S(1)}) custom-call(s32[2,16]{1,0:T(2,128)S(1)} %copy-done, f32[2,16]{1,0:T(2,128)S(1)} %copy-done.1, f32[2,16]{1,0:T(2,128)S(1)} %copy-done.2), custom_call_target="tpu_custom_call" | custom-call | flops 7864320 | bytes 524288 | tf_op jit(solution)/shard_map/taper_tables/pallas_call | solution.py:324
  47.1 5.7 %filter_plan.1 = (f32[33,24,128]{2,1,0:T(8,128)S(1)}, f32[33,24,128]{2,1,0:T(8,128)S(1)}, f32[128,128]{1,0:T(8,128)S(1)}, f32[128,128]{1,0:T(8,128)S(1)}, f32[12...) custom-call(f32[33,32,128]{2,1,0:T(8,128)S(1)} %get-tuple-element.37, ...), custom_call_target="tpu_custom_call" | custom-call | flops 20000000 | bytes 1048576 | tf_op jit(solution)/shard_map/filter_plan/pallas_call | solution.py:439
  53.8 2.2 %collective-permute-start.18 = (f32[128,128]{1,0:T(8,128)S(1)}, f32[128,128]{1,0:T(8,128)S(1)}, u32[]{:S(2)}, u32[]{:S(2)}) collective-permute-start(f32[128,128]{1,0:T(8,128)S(1)} %get-tuple-element.61), channel_id=1, source_target_pairs={{0,8},{4,12},{8,0},{12,4},{16,24},{20,28},{24,16},{28,20},{1,9},{5... | collective-permute-start | bytes 196616 | tf_op jit(solution)/shard_map/ppermute | solution.py:548
  56.9 2.2 %collective-permute-start.20 = (f32[128,128]{1,0:T(8,128)S(1)}, f32[128,128]{1,0:T(8,128)S(1)}, u32[]{:S(2)}, u32[]{:S(2)}) collective-permute-start(f32[128,128]{1,0:T(8,128)S(1)} %get-tuple-element.63), channel_id=1, source_target_pairs={{0,16},{4,20},{8,24},{12,28},{16,0},{20,4},{24,8},{28,12},{1,17},{... | collective-permute-start | bytes 196616 | tf_op jit(solution)/shard_map/ppermute | solution.py:548
  59.1 3.9 %settle.1 = (f32[192,128]{1,0:T(8,128)S(1)}, f32[192,128]{1,0:T(8,128)S(1)}, f32[192,128]{1,0:T(8,128)S(1)}, f32[192,128]{1,0:T(8,128)S(1)}, f32[192,128]{1,0:T(...) custom-call(s32[8,128]{1,0:T(8,128)S(1)} %get-tuple-element.36.lists_ref, ...), custom_call_target="tpu_custom_call" | custom-call | flops 25952256 | bytes 1572864 | tf_op jit(solution)/shard_map/settle/pallas_call | solution.py:467
  63.6 3.6 %collective-permute-start.21 = (f32[128,128]{1,0:T(8,128)S(1)}, f32[128,128]{1,0:T(8,128)S(1)}, u32[]{:S(2)}, u32[]{:S(2)}) collective-permute-start(f32[128,128]{1,0:T(8,128)S(1)} %get-tuple-element.64), channel_id=1, source_target_pairs={{0,20},{4,16},{8,28},{12,24},{16,4},{20,0},{24,12},{28,8},{1,21},{... | collective-permute-start | bytes 196616 | tf_op jit(solution)/shard_map/ppermute | solution.py:548
  67.2 1.6 %collective-permute-start.22 = (f32[128,128]{1,0:T(8,128)S(1)}, f32[128,128]{1,0:T(8,128)S(1)}, u32[]{:S(2)}, u32[]{:S(2)}) collective-permute-start(f32[128,128]{1,0:T(8,128)S(1)} %get-tuple-element.65), channel_id=1, source_target_pairs={{0,24},{4,28},{8,16},{12,20},{16,8},{20,12},{24,0},{28,4},{1,25},{... | collective-permute-start | bytes 196616 | tf_op jit(solution)/shard_map/ppermute | solution.py:548
  68.9 2.3 %collective-permute-start.23 = (f32[128,128]{1,0:T(8,128)S(1)}, f32[128,128]{1,0:T(8,128)S(1)}, u32[]{:S(2)}, u32[]{:S(2)}) collective-permute-start(f32[128,128]{1,0:T(8,128)S(1)} %get-tuple-element.66), channel_id=1, source_target_pairs={{0,28},{4,24},{8,20},{12,16},{16,12},{20,8},{24,4},{28,0},{1,29},{... | collective-permute-start | bytes 196616 | tf_op jit(solution)/shard_map/ppermute | solution.py:548
  74.0 3.5 %collective-permute-start.13 = (f32[192,128]{1,0:T(8,128)S(1)}, f32[192,128]{1,0:T(8,128)S(1)}, u32[]{:S(2)}, u32[]{:S(2)}) collective-permute-start(f32[192,128]{1,0:T(8,128)S(1)} %get-tuple-element.55), channel_id=1, source_target_pairs={{0,16},{4,20},{8,24},{12,28},{16,0},{20,4},{24,8},{28,12},{1,17},{... | collective-permute-start | bytes 294920 | tf_op jit(solution)/shard_map/ppermute | solution.py:548
  77.6 2.8 %collective-permute-start.14 = (f32[192,128]{1,0:T(8,128)S(1)}, f32[192,128]{1,0:T(8,128)S(1)}, u32[]{:S(2)}, u32[]{:S(2)}) collective-permute-start(f32[192,128]{1,0:T(8,128)S(1)} %get-tuple-element.56), channel_id=1, source_target_pairs={{0,20},{4,16},{8,28},{12,24},{16,4},{20,0},{24,12},{28,8},{1,21},{... | collective-permute-start | bytes 294920 | tf_op jit(solution)/shard_map/ppermute | solution.py:548
  80.4 1.9 %collective-permute-start.15 = (f32[192,128]{1,0:T(8,128)S(1)}, f32[192,128]{1,0:T(8,128)S(1)}, u32[]{:S(2)}, u32[]{:S(2)}) collective-permute-start(f32[192,128]{1,0:T(8,128)S(1)} %get-tuple-element.57), channel_id=1, source_target_pairs={{0,24},{4,28},{8,16},{12,20},{16,8},{20,12},{24,0},{28,4},{1,25},{... | collective-permute-start | bytes 294920 | tf_op jit(solution)/shard_map/ppermute | solution.py:548
  84.6 4.0 %collective-permute-done.13.refs_4_ = f32[192,128]{1,0:T(8,128)S(1)} collective-permute-done((f32[192,128]{1,0:T(8,128)S(1)}, f32[192,128]{1,0:T(8,128)S(1)}, u32[]{:S(2)}, u32[]{:S(2)}) %collective-permute-start.13) | collective-permute-done | bytes 98336 | tf_op jit(solution)/shard_map/ppermute | solution.py:548
  88.6 2.1 %collective-permute-done.14.refs_5_ = f32[192,128]{1,0:T(8,128)S(1)} collective-permute-done((f32[192,128]{1,0:T(8,128)S(1)}, f32[192,128]{1,0:T(8,128)S(1)}, u32[]{:S(2)}, u32[]{:S(2)}) %collective-permute-start.14) | collective-permute-done | bytes 98336 | tf_op jit(solution)/shard_map/ppermute | solution.py:548
  (41 shorter events, 11.4 us)
Async XLA Ops:
  4.0 55.1 %all-to-all-start = ((f32[8,192,128]{2,1,0:T(8,128)}), f32[8,192,128]{2,1,0:T(8,128)S(1)}, u32[]{:S(2)}, u32[]{:S(2)}) async-start(f32[8,192,128]{2,1,0:T(8,128)} %get-tuple-element.50), calls=%async_computation | async-start | bytes 1572864 | tf_op jit(solution)/shard_map/all_to_all | solution.py:545
  11.4 8.8 %collective-permute-start = (f32[136,128]{1,0:T(8,128)S(1)}, f32[136,128]{1,0:T(8,128)S(1)}, u32[]{:S(2)}, u32[]{:S(2)}) collective-permute-start(f32[136,128]{1,0:T(8,128)S(1)} %get-tuple-element.41), channel_id=1, source_target_pairs={{0,4},{4,0},{8,12},{12,8},{16,20},{20,16},{24,28},{28,24},{1,5},{5... | collective-permute-start | bytes 208904 | tf_op jit(solution)/shard_map/ppermute | solution.py:548
  13.5 13.4 %collective-permute-start.1 = (f32[136,128]{1,0:T(8,128)S(1)}, f32[136,128]{1,0:T(8,128)S(1)}, u32[]{:S(2)}, u32[]{:S(2)}) collective-permute-start(f32[136,128]{1,0:T(8,128)S(1)} %get-tuple-element.42), channel_id=1, source_target_pairs={{0,8},{4,12},{8,0},{12,4},{16,24},{20,28},{24,16},{28,20},{1,9},{5... | collective-permute-start | bytes 208904 | tf_op jit(solution)/shard_map/ppermute | solution.py:548
  14.9 16.7 %collective-permute-start.2 = (f32[136,128]{1,0:T(8,128)S(1)}, f32[136,128]{1,0:T(8,128)S(1)}, u32[]{:S(2)}, u32[]{:S(2)}) collective-permute-start(f32[136,128]{1,0:T(8,128)S(1)} %get-tuple-element.43), channel_id=1, source_target_pairs={{0,12},{4,8},{8,4},{12,0},{16,28},{20,24},{24,20},{28,16},{1,13},{... | collective-permute-start | bytes 208904 | tf_op jit(solution)/shard_map/ppermute | solution.py:548
  14.9 25.5 %collective-permute-start.3 = (f32[136,128]{1,0:T(8,128)S(1)}, f32[136,128]{1,0:T(8,128)S(1)}, u32[]{:S(2)}, u32[]{:S(2)}) collective-permute-start(f32[136,128]{1,0:T(8,128)S(1)} %get-tuple-element.44), channel_id=1, source_target_pairs={{0,16},{4,20},{8,24},{12,28},{16,0},{20,4},{24,8},{28,12},{1,17},{... | collective-permute-start | bytes 208904 | tf_op jit(solution)/shard_map/ppermute | solution.py:548
  17.8 24.5 %collective-permute-start.4 = (f32[136,128]{1,0:T(8,128)S(1)}, f32[136,128]{1,0:T(8,128)S(1)}, u32[]{:S(2)}, u32[]{:S(2)}) collective-permute-start(f32[136,128]{1,0:T(8,128)S(1)} %get-tuple-element.45), channel_id=1, source_target_pairs={{0,20},{4,16},{8,28},{12,24},{16,4},{20,0},{24,12},{28,8},{1,21},{... | collective-permute-start | bytes 208904 | tf_op jit(solution)/shard_map/ppermute | solution.py:548
  20.3 22.1 %collective-permute-start.5 = (f32[136,128]{1,0:T(8,128)S(1)}, f32[136,128]{1,0:T(8,128)S(1)}, u32[]{:S(2)}, u32[]{:S(2)}) collective-permute-start(f32[136,128]{1,0:T(8,128)S(1)} %get-tuple-element.46), channel_id=1, source_target_pairs={{0,24},{4,28},{8,16},{12,20},{16,8},{20,12},{24,0},{28,4},{1,25},{... | collective-permute-start | bytes 208904 | tf_op jit(solution)/shard_map/ppermute | solution.py:548
  26.8 15.5 %collective-permute-start.6 = (f32[136,128]{1,0:T(8,128)S(1)}, f32[136,128]{1,0:T(8,128)S(1)}, u32[]{:S(2)}, u32[]{:S(2)}) collective-permute-start(f32[136,128]{1,0:T(8,128)S(1)} %get-tuple-element.47), channel_id=1, source_target_pairs={{0,28},{4,24},{8,20},{12,16},{16,12},{20,8},{24,4},{28,0},{1,29},{... | collective-permute-start | bytes 208904 | tf_op jit(solution)/shard_map/ppermute | solution.py:548
  42.4 4.6 %collective-permute-start.9 = (f32[16,128]{1,0:T(8,128)S(1)}, f32[16,128]{1,0:T(8,128)S(1)}, u32[]{:S(2)}, u32[]{:S(2)}) collective-permute-start(f32[16,128]{1,0:T(8,128)S(1)} %pad_maximum_fusion.refs_0_), channel_id=1, source_target_pairs={{0,3},{1,0},{2,1},{3,2},{4,7},{5,4},{6,5},{7,6},{8,11},{9,8},{10,9... | collective-permute-start | bytes 24584 | tf_op jit(solution)/shard_map/ppermute | solution.py:566
  42.5 4.6 %collective-permute-start.8 = (f32[16,128]{1,0:T(8,128)S(1)}, f32[16,128]{1,0:T(8,128)S(1)}, u32[]{:S(2)}, u32[]{:S(2)}) collective-permute-start(f32[16,128]{1,0:T(8,128)S(1)} %pad_maximum_fusion.refs_0_), channel_id=1, source_target_pairs={{0,2},{1,3},{2,0},{3,1},{4,6},{5,7},{6,4},{7,5},{8,10},{9,11},{10,... | collective-permute-start | bytes 24584 | tf_op jit(solution)/shard_map/ppermute | solution.py:566
  52.8 10.3 %collective-permute-start.17 = (f32[128,128]{1,0:T(8,128)S(1)}, f32[128,128]{1,0:T(8,128)S(1)}, u32[]{:S(2)}, u32[]{:S(2)}) collective-permute-start(f32[128,128]{1,0:T(8,128)S(1)} %get-tuple-element.60), channel_id=1, source_target_pairs={{0,4},{4,0},{8,12},{12,8},{16,20},{20,16},{24,28},{28,24},{1,5},{5... | collective-permute-start | bytes 196616 | tf_op jit(solution)/shard_map/ppermute | solution.py:548
  53.8 9.7 %collective-permute-start.18 = (f32[128,128]{1,0:T(8,128)S(1)}, f32[128,128]{1,0:T(8,128)S(1)}, u32[]{:S(2)}, u32[]{:S(2)}) collective-permute-start(f32[128,128]{1,0:T(8,128)S(1)} %get-tuple-element.61), channel_id=1, source_target_pairs={{0,8},{4,12},{8,0},{12,4},{16,24},{20,28},{24,16},{28,20},{1,9},{5... | collective-permute-start | bytes 196616 | tf_op jit(solution)/shard_map/ppermute | solution.py:548
  56.0 11.2 %collective-permute-start.19 = (f32[128,128]{1,0:T(8,128)S(1)}, f32[128,128]{1,0:T(8,128)S(1)}, u32[]{:S(2)}, u32[]{:S(2)}) collective-permute-start(f32[128,128]{1,0:T(8,128)S(1)} %get-tuple-element.62), channel_id=1, source_target_pairs={{0,12},{4,8},{8,4},{12,0},{16,28},{20,24},{24,20},{28,16},{1,13},{... | collective-permute-start | bytes 196616 | tf_op jit(solution)/shard_map/ppermute | solution.py:548
  56.9 12.0 %collective-permute-start.20 = (f32[128,128]{1,0:T(8,128)S(1)}, f32[128,128]{1,0:T(8,128)S(1)}, u32[]{:S(2)}, u32[]{:S(2)}) collective-permute-start(f32[128,128]{1,0:T(8,128)S(1)} %get-tuple-element.63), channel_id=1, source_target_pairs={{0,16},{4,20},{8,24},{12,28},{16,0},{20,4},{24,8},{28,12},{1,17},{... | collective-permute-start | bytes 196616 | tf_op jit(solution)/shard_map/ppermute | solution.py:548
  62.9 17.4 %collective-permute-start.10 = (f32[192,128]{1,0:T(8,128)S(1)}, f32[192,128]{1,0:T(8,128)S(1)}, u32[]{:S(2)}, u32[]{:S(2)}) collective-permute-start(f32[192,128]{1,0:T(8,128)S(1)} %get-tuple-element.52), channel_id=1, source_target_pairs={{0,4},{4,0},{8,12},{12,8},{16,20},{20,16},{24,28},{28,24},{1,5},{5... | collective-permute-start | bytes 294920 | tf_op jit(solution)/shard_map/ppermute | solution.py:548
  63.1 19.2 %collective-permute-start.11 = (f32[192,128]{1,0:T(8,128)S(1)}, f32[192,128]{1,0:T(8,128)S(1)}, u32[]{:S(2)}, u32[]{:S(2)}) collective-permute-start(f32[192,128]{1,0:T(8,128)S(1)} %get-tuple-element.53), channel_id=1, source_target_pairs={{0,8},{4,12},{8,0},{12,4},{16,24},{20,28},{24,16},{28,20},{1,9},{5... | collective-permute-start | bytes 294920 | tf_op jit(solution)/shard_map/ppermute | solution.py:548
  63.6 8.8 %collective-permute-start.21 = (f32[128,128]{1,0:T(8,128)S(1)}, f32[128,128]{1,0:T(8,128)S(1)}, u32[]{:S(2)}, u32[]{:S(2)}) collective-permute-start(f32[128,128]{1,0:T(8,128)S(1)} %get-tuple-element.64), channel_id=1, source_target_pairs={{0,20},{4,16},{8,28},{12,24},{16,4},{20,0},{24,12},{28,8},{1,21},{... | collective-permute-start | bytes 196616 | tf_op jit(solution)/shard_map/ppermute | solution.py:548
  67.2 6.8 %collective-permute-start.22 = (f32[128,128]{1,0:T(8,128)S(1)}, f32[128,128]{1,0:T(8,128)S(1)}, u32[]{:S(2)}, u32[]{:S(2)}) collective-permute-start(f32[128,128]{1,0:T(8,128)S(1)} %get-tuple-element.65), channel_id=1, source_target_pairs={{0,24},{4,28},{8,16},{12,20},{16,8},{20,12},{24,0},{28,4},{1,25},{... | collective-permute-start | bytes 196616 | tf_op jit(solution)/shard_map/ppermute | solution.py:548
  68.9 8.7 %collective-permute-start.23 = (f32[128,128]{1,0:T(8,128)S(1)}, f32[128,128]{1,0:T(8,128)S(1)}, u32[]{:S(2)}, u32[]{:S(2)}) collective-permute-start(f32[128,128]{1,0:T(8,128)S(1)} %get-tuple-element.66), channel_id=1, source_target_pairs={{0,28},{4,24},{8,20},{12,16},{16,12},{20,8},{24,4},{28,0},{1,29},{... | collective-permute-start | bytes 196616 | tf_op jit(solution)/shard_map/ppermute | solution.py:548
  72.4 12.2 %collective-permute-start.12 = (f32[192,128]{1,0:T(8,128)S(1)}, f32[192,128]{1,0:T(8,128)S(1)}, u32[]{:S(2)}, u32[]{:S(2)}) collective-permute-start(f32[192,128]{1,0:T(8,128)S(1)} %get-tuple-element.54), channel_id=1, source_target_pairs={{0,12},{4,8},{8,4},{12,0},{16,28},{20,24},{24,20},{28,16},{1,13},{... | collective-permute-start | bytes 294920 | tf_op jit(solution)/shard_map/ppermute | solution.py:548
  74.0 14.6 %collective-permute-start.13 = (f32[192,128]{1,0:T(8,128)S(1)}, f32[192,128]{1,0:T(8,128)S(1)}, u32[]{:S(2)}, u32[]{:S(2)}) collective-permute-start(f32[192,128]{1,0:T(8,128)S(1)} %get-tuple-element.55), channel_id=1, source_target_pairs={{0,16},{4,20},{8,24},{12,28},{16,0},{20,4},{24,8},{28,12},{1,17},{... | collective-permute-start | bytes 294920 | tf_op jit(solution)/shard_map/ppermute | solution.py:548
  77.6 13.1 %collective-permute-start.14 = (f32[192,128]{1,0:T(8,128)S(1)}, f32[192,128]{1,0:T(8,128)S(1)}, u32[]{:S(2)}, u32[]{:S(2)}) collective-permute-start(f32[192,128]{1,0:T(8,128)S(1)} %get-tuple-element.56), channel_id=1, source_target_pairs={{0,20},{4,16},{8,28},{12,24},{16,4},{20,0},{24,12},{28,8},{1,21},{... | collective-permute-start | bytes 294920 | tf_op jit(solution)/shard_map/ppermute | solution.py:548
  80.4 10.3 %collective-permute-start.15 = (f32[192,128]{1,0:T(8,128)S(1)}, f32[192,128]{1,0:T(8,128)S(1)}, u32[]{:S(2)}, u32[]{:S(2)}) collective-permute-start(f32[192,128]{1,0:T(8,128)S(1)} %get-tuple-element.57), channel_id=1, source_target_pairs={{0,24},{4,28},{8,16},{12,20},{16,8},{20,12},{24,0},{28,4},{1,25},{... | collective-permute-start | bytes 294920 | tf_op jit(solution)/shard_map/ppermute | solution.py:548
  82.3 8.4 %collective-permute-start.16 = (f32[192,128]{1,0:T(8,128)S(1)}, f32[192,128]{1,0:T(8,128)S(1)}, u32[]{:S(2)}, u32[]{:S(2)}) collective-permute-start(f32[192,128]{1,0:T(8,128)S(1)} %get-tuple-element.58), channel_id=1, source_target_pairs={{0,28},{4,24},{8,20},{12,16},{16,12},{20,8},{24,4},{28,0},{1,29},{... | collective-permute-start | bytes 294920 | tf_op jit(solution)/shard_map/ppermute | solution.py:548
  (4 other events, 123.8 us)
where the time goes:
time: 91.9 us; the launch traced here: 91.7 us
  starting transfers between devices  48.9 us (53%)
  waiting for transfers between devices  24.5 us (27%)
  Pallas kernels  18.1 us (20%)
    ppermute x21, starting transfers between devices, exchange(): got[j] = lax.ppermute(blocks[j], 'mem', [(i, i ^ j) for i in range(n)])  39.7 us
    ppermute x21, waiting for transfers between devices, exchange(): got[j] = lax.ppermute(blocks[j], 'mem', [(i, i ^ j) for i in range(n)])  24.4 us
    all_to_all x1, starting transfers between devices, exchange(): lax.all_to_all(blocks[0], 'mem', split_axis=0, concat_axis=0, tiled=True)  7.45 us
    pallas_call x1, Pallas kernels, filter_plan(): pl.pallas_call(functools.partial(plan_kernel, n, mem_dev, count, len(seen...  5.69 us
    pallas_call x1, Pallas kernels, forecast(): pl.pallas_call(functools.partial(forecast_kernel, parts, n), in_specs=[pl...  3.93 us
    pallas_call x1, Pallas kernels, settle(): pl.pallas_call(functools.partial(settle_kernel, n, mem_dev, count, depth,...  3.86 us
    pallas_call x1, Pallas kernels, taper_tables(): pl.pallas_call(functools.partial(taper_kernel, nx, block), in_specs=[SMEM...  2.83 us
  transfers between devices with their start and end apart: 25, of which 9 were waited for; matrix products, arithmetic and copies ran while one was open for 0% of the time, Pallas kernels for 14%

commit v1 on v0

--- a/solution.py
+++ b/solution.py
@@ -102,7 +102,7 @@
         pltpu.make_async_copy(cells_hbm, cells, small.at[1]),
         pltpu.make_async_copy(slabs_hbm, slabs, small.at[2]),
     )
-    for copy in [*loads(0), *lists] + [copy for c in range(1, len(parts)) for copy in loads(c)]:
+    for copy in [*lists, *loads(0)] + [copy for c in range(1, len(parts)) for copy in loads(c)]:
         copy.start()
     for copy in lists:
         copy.wait()
@@ -531,20 +531,18 @@
     )(*recv, *extra)
 
 
-def order_of(n, first):
+def order_of(n, near_first=False):
     far, near = list(range(n // 2, n)), list(range(2, n // 2)) + [1]
-    if first == "far":
-        return far + near
-    if first == "near":
+    if near_first:
         return near + far
     return [j for pair in zip(far, near) for j in pair] + far[len(near) :]
 
 
-def exchange(blocks, n, whole, first):
+def exchange(blocks, n, whole, near_first=False):
     if whole:
         return [lax.all_to_all(blocks[0], "mem", split_axis=0, concat_axis=0, tiled=True)]
     got = {}
-    for j in order_of(n, first):
+    for j in order_of(n, near_first):
         got[j] = lax.ppermute(blocks[j], "mem", [(i, i ^ j) for i in range(n)])
     return blocks[:1] + [got[j] for j in range(1, n)]
 
@@ -558,7 +556,7 @@
     sends = forecast(parts, n, obs_cells, obs_slabs, spread, x, cv, ch)
     states = []
     for c, blocks in enumerate(sends):
-        states.append(exchange(blocks, n, parts[c][2], "far"))
+        states.append(exchange(blocks, n, parts[c][2]))
     per = TILE // mem_dev
     seen = [s[mem_dev * parts[0][1] * depth :, :] for s in states[0]]
     seen = jnp.concatenate([sum(seen[g : g + per]) for g in range(0, n, per)])
@@ -573,7 +571,7 @@
             tables, new = filter_plan(mem_dev, count, places, tiles, state)
         else:
             new = settle(n, mem_dev, count, whole, places, tables, state)
-        back = exchange(list(new), n, False, "near" if c == 0 else "turns")
+        back = exchange(list(new), n, False, near_first=c == 0)
         result = assemble(n, start, count, back, x.shape, result)
     return result
 

time: 91.9 us -> 91.9 us (level)
  no operation moved by 1% of the time
where the time goes in v1:
time: 91.9 us; the launch traced here: 91.7 us
  starting transfers between devices  48.9 us (53%)
  waiting for transfers between devices  24.5 us (27%)
  Pallas kernels  18.1 us (20%)
    ppermute x21, starting transfers between devices, exchange(): got[j] = lax.ppermute(blocks[j], 'mem', [(i, i ^ j) for i in range(n)])  39.7 us
    ppermute x21, waiting for transfers between devices, exchange(): got[j] = lax.ppermute(blocks[j], 'mem', [(i, i ^ j) for i in range(n)])  24.4 us
    all_to_all x1, starting transfers between devices, exchange(): lax.all_to_all(blocks[0], 'mem', split_axis=0, concat_axis=0, tiled=True)  7.45 us
    pallas_call x1, Pallas kernels, filter_plan(): pl.pallas_call(functools.partial(plan_kernel, n, mem_dev, count, len(seen...  5.69 us
    pallas_call x1, Pallas kernels, forecast(): pl.pallas_call(functools.partial(forecast_kernel, parts, n), in_specs=[pl...  3.93 us
    pallas_call x1, Pallas kernels, settle(): pl.pallas_call(functools.partial(settle_kernel, n, mem_dev, count, depth,...  3.86 us
    pallas_call x1, Pallas kernels, taper_tables(): pl.pallas_call(functools.partial(taper_kernel, nx, block), in_specs=[SMEM...  2.83 us
  transfers between devices with their start and end apart: 25, of which 9 were waited for; matrix products, arithmetic and copies ran while one was open for 0% of the time, Pallas kernels for 14%

profile of v1, /device:TPU:0, one launch (start us, length us, event | category | flops | bytes accessed | tf_op | source)
XLA Modules:
  0.0 91.7 jit_solution(10089080241784694560)
XLA Ops:
  0.0 3.9 %forecast.1 = (f32[136,128]{1,0:T(8,128)S(1)}, f32[136,128]{1,0:T(8,128)S(1)}, f32[136,128]{1,0:T(8,128)S(1)}, f32[136,128]{1,0:T(8,128)S(1)}, f32[136,128]{1,0:...) custom-call(s32[2,16]{1,0:T(2,128)} %cells_hbm.1, ...), custom_call_target="tpu_custom_call" | custom-call | flops 19660800 | bytes 3932160 | tf_op jit(solution)/shard_map/forecast/pallas_call | solution.py:234
  4.0 7.5 %all-to-all-start = ((f32[8,192,128]{2,1,0:T(8,128)}), f32[8,192,128]{2,1,0:T(8,128)S(1)}, u32[]{:S(2)}, u32[]{:S(2)}) async-start(f32[8,192,128]{2,1,0:T(8,128)} %get-tuple-element.50), calls=%async_computation | async-start | bytes 1572864 | tf_op jit(solution)/shard_map/all_to_all | solution.py:543
  11.4 2.0 %collective-permute-start = (f32[136,128]{1,0:T(8,128)S(1)}, f32[136,128]{1,0:T(8,128)S(1)}, u32[]{:S(2)}, u32[]{:S(2)}) collective-permute-start(f32[136,128]{1,0:T(8,128)S(1)} %get-tuple-element.41), channel_id=1, source_target_pairs={{0,4},{4,0},{8,12},{12,8},{16,20},{20,16},{24,28},{28,24},{1,5},{5... | collective-permute-start | bytes 208904 | tf_op jit(solution)/shard_map/ppermute | solution.py:546
  13.4 1.5 %collective-permute-start.1 = (f32[136,128]{1,0:T(8,128)S(1)}, f32[136,128]{1,0:T(8,128)S(1)}, u32[]{:S(2)}, u32[]{:S(2)}) collective-permute-start(f32[136,128]{1,0:T(8,128)S(1)} %get-tuple-element.42), channel_id=1, source_target_pairs={{0,8},{4,12},{8,0},{12,4},{16,24},{20,28},{24,16},{28,20},{1,9},{5... | collective-permute-start | bytes 208904 | tf_op jit(solution)/shard_map/ppermute | solution.py:546
  14.9 2.9 %collective-permute-start.3 = (f32[136,128]{1,0:T(8,128)S(1)}, f32[136,128]{1,0:T(8,128)S(1)}, u32[]{:S(2)}, u32[]{:S(2)}) collective-permute-start(f32[136,128]{1,0:T(8,128)S(1)} %get-tuple-element.44), channel_id=1, source_target_pairs={{0,16},{4,20},{8,24},{12,28},{16,0},{20,4},{24,8},{28,12},{1,17},{... | collective-permute-start | bytes 208904 | tf_op jit(solution)/shard_map/ppermute | solution.py:546
  20.3 2.4 %collective-permute-start.5 = (f32[136,128]{1,0:T(8,128)S(1)}, f32[136,128]{1,0:T(8,128)S(1)}, u32[]{:S(2)}, u32[]{:S(2)}) collective-permute-start(f32[136,128]{1,0:T(8,128)S(1)} %get-tuple-element.46), channel_id=1, source_target_pairs={{0,24},{4,28},{8,16},{12,20},{16,8},{20,12},{24,0},{28,4},{1,25},{... | collective-permute-start | bytes 208904 | tf_op jit(solution)/shard_map/ppermute | solution.py:546
  22.7 4.2 %collective-permute-done.1.refs_6_ = f32[136,128]{1,0:T(8,128)S(1)} collective-permute-done((f32[136,128]{1,0:T(8,128)S(1)}, f32[136,128]{1,0:T(8,128)S(1)}, u32[]{:S(2)}, u32[]{:S(2)}) %collective-permute-start.1) | collective-permute-done | bytes 69664 | tf_op jit(solution)/shard_map/ppermute | solution.py:546
  26.8 4.7 %collective-permute-start.6 = (f32[136,128]{1,0:T(8,128)S(1)}, f32[136,128]{1,0:T(8,128)S(1)}, u32[]{:S(2)}, u32[]{:S(2)}) collective-permute-start(f32[136,128]{1,0:T(8,128)S(1)} %get-tuple-element.47), channel_id=1, source_target_pairs={{0,28},{4,24},{8,20},{12,16},{16,12},{20,8},{24,4},{28,0},{1,29},{... | collective-permute-start | bytes 208904 | tf_op jit(solution)/shard_map/ppermute | solution.py:546
  31.6 8.8 %collective-permute-done.3.refs_8_ = f32[136,128]{1,0:T(8,128)S(1)} collective-permute-done((f32[136,128]{1,0:T(8,128)S(1)}, f32[136,128]{1,0:T(8,128)S(1)}, u32[]{:S(2)}, u32[]{:S(2)}) %collective-permute-start.3) | collective-permute-done | bytes 69664 | tf_op jit(solution)/shard_map/ppermute | solution.py:546
  40.4 2.0 %collective-permute-done.4.refs_9_ = f32[136,128]{1,0:T(8,128)S(1)} collective-permute-done((f32[136,128]{1,0:T(8,128)S(1)}, f32[136,128]{1,0:T(8,128)S(1)}, u32[]{:S(2)}, u32[]{:S(2)}) %collective-permute-start.4) | collective-permute-done | bytes 69664 | tf_op jit(solution)/shard_map/ppermute | solution.py:546
  42.5 1.6 %collective-permute-start.8 = (f32[16,128]{1,0:T(8,128)S(1)}, f32[16,128]{1,0:T(8,128)S(1)}, u32[]{:S(2)}, u32[]{:S(2)}) collective-permute-start(f32[16,128]{1,0:T(8,128)S(1)} %pad_maximum_fusion.refs_0_), channel_id=1, source_target_pairs={{0,2},{1,3},{2,0},{3,1},{4,6},{5,7},{6,4},{7,5},{8,10},{9,11},{10,... | collective-permute-start | bytes 24584 | tf_op jit(solution)/shard_map/ppermute | solution.py:564
  44.2 2.8 %taper_tables.1 = (f32[33,32,128]{2,1,0:T(8,128)S(1)}, f32[32,128]{1,0:T(8,128)S(1)}, f32[32,8,128]{2,1,0:T(8,128)S(1)}, s32[8,128]{1,0:T(8,128)S(1)}) custom-call(s32[2,16]{1,0:T(2,128)S(1)} %copy-done, f32[2,16]{1,0:T(2,128)S(1)} %copy-done.1, f32[2,16]{1,0:T(2,128)S(1)} %copy-done.2), custom_call_target="tpu_custom_call" | custom-call | flops 7864320 | bytes 524288 | tf_op jit(solution)/shard_map/taper_tables/pallas_call | solution.py:324
  47.1 5.7 %filter_plan.1 = (f32[33,24,128]{2,1,0:T(8,128)S(1)}, f32[33,24,128]{2,1,0:T(8,128)S(1)}, f32[128,128]{1,0:T(8,128)S(1)}, f32[128,128]{1,0:T(8,128)S(1)}, f32[12...) custom-call(f32[33,32,128]{2,1,0:T(8,128)S(1)} %get-tuple-element.37, ...), custom_call_target="tpu_custom_call" | custom-call | flops 20000000 | bytes 1048576 | tf_op jit(solution)/shard_map/filter_plan/pallas_call | solution.py:439
  53.8 2.2 %collective-permute-start.18 = (f32[128,128]{1,0:T(8,128)S(1)}, f32[128,128]{1,0:T(8,128)S(1)}, u32[]{:S(2)}, u32[]{:S(2)}) collective-permute-start(f32[128,128]{1,0:T(8,128)S(1)} %get-tuple-element.61), channel_id=1, source_target_pairs={{0,8},{4,12},{8,0},{12,4},{16,24},{20,28},{24,16},{28,20},{1,9},{5... | collective-permute-start | bytes 196616 | tf_op jit(solution)/shard_map/ppermute | solution.py:546
  56.9 2.2 %collective-permute-start.20 = (f32[128,128]{1,0:T(8,128)S(1)}, f32[128,128]{1,0:T(8,128)S(1)}, u32[]{:S(2)}, u32[]{:S(2)}) collective-permute-start(f32[128,128]{1,0:T(8,128)S(1)} %get-tuple-element.63), channel_id=1, source_target_pairs={{0,16},{4,20},{8,24},{12,28},{16,0},{20,4},{24,8},{28,12},{1,17},{... | collective-permute-start | bytes 196616 | tf_op jit(solution)/shard_map/ppermute | solution.py:546
  59.1 3.9 %settle.1 = (f32[192,128]{1,0:T(8,128)S(1)}, f32[192,128]{1,0:T(8,128)S(1)}, f32[192,128]{1,0:T(8,128)S(1)}, f32[192,128]{1,0:T(8,128)S(1)}, f32[192,128]{1,0:T(...) custom-call(s32[8,128]{1,0:T(8,128)S(1)} %get-tuple-element.36.lists_ref, ...), custom_call_target="tpu_custom_call" | custom-call | flops 25952256 | bytes 1572864 | tf_op jit(solution)/shard_map/settle/pallas_call | solution.py:467
  63.6 3.6 %collective-permute-start.21 = (f32[128,128]{1,0:T(8,128)S(1)}, f32[128,128]{1,0:T(8,128)S(1)}, u32[]{:S(2)}, u32[]{:S(2)}) collective-permute-start(f32[128,128]{1,0:T(8,128)S(1)} %get-tuple-element.64), channel_id=1, source_target_pairs={{0,20},{4,16},{8,28},{12,24},{16,4},{20,0},{24,12},{28,8},{1,21},{... | collective-permute-start | bytes 196616 | tf_op jit(solution)/shard_map/ppermute | solution.py:546
  67.2 1.6 %collective-permute-start.22 = (f32[128,128]{1,0:T(8,128)S(1)}, f32[128,128]{1,0:T(8,128)S(1)}, u32[]{:S(2)}, u32[]{:S(2)}) collective-permute-start(f32[128,128]{1,0:T(8,128)S(1)} %get-tuple-element.65), channel_id=1, source_target_pairs={{0,24},{4,28},{8,16},{12,20},{16,8},{20,12},{24,0},{28,4},{1,25},{... | collective-permute-start | bytes 196616 | tf_op jit(solution)/shard_map/ppermute | solution.py:546
  68.8 2.3 %collective-permute-start.23 = (f32[128,128]{1,0:T(8,128)S(1)}, f32[128,128]{1,0:T(8,128)S(1)}, u32[]{:S(2)}, u32[]{:S(2)}) collective-permute-start(f32[128,128]{1,0:T(8,128)S(1)} %get-tuple-element.66), channel_id=1, source_target_pairs={{0,28},{4,24},{8,20},{12,16},{16,12},{20,8},{24,4},{28,0},{1,29},{... | collective-permute-start | bytes 196616 | tf_op jit(solution)/shard_map/ppermute | solution.py:546
  74.0 3.5 %collective-permute-start.13 = (f32[192,128]{1,0:T(8,128)S(1)}, f32[192,128]{1,0:T(8,128)S(1)}, u32[]{:S(2)}, u32[]{:S(2)}) collective-permute-start(f32[192,128]{1,0:T(8,128)S(1)} %get-tuple-element.55), channel_id=1, source_target_pairs={{0,16},{4,20},{8,24},{12,28},{16,0},{20,4},{24,8},{28,12},{1,17},{... | collective-permute-start | bytes 294920 | tf_op jit(solution)/shard_map/ppermute | solution.py:546
  77.6 2.8 %collective-permute-start.14 = (f32[192,128]{1,0:T(8,128)S(1)}, f32[192,128]{1,0:T(8,128)S(1)}, u32[]{:S(2)}, u32[]{:S(2)}) collective-permute-start(f32[192,128]{1,0:T(8,128)S(1)} %get-tuple-element.56), channel_id=1, source_target_pairs={{0,20},{4,16},{8,28},{12,24},{16,4},{20,0},{24,12},{28,8},{1,21},{... | collective-permute-start | bytes 294920 | tf_op jit(solution)/shard_map/ppermute | solution.py:546
  80.4 1.9 %collective-permute-start.15 = (f32[192,128]{1,0:T(8,128)S(1)}, f32[192,128]{1,0:T(8,128)S(1)}, u32[]{:S(2)}, u32[]{:S(2)}) collective-permute-start(f32[192,128]{1,0:T(8,128)S(1)} %get-tuple-element.57), channel_id=1, source_target_pairs={{0,24},{4,28},{8,16},{12,20},{16,8},{20,12},{24,0},{28,4},{1,25},{... | collective-permute-start | bytes 294920 | tf_op jit(solution)/shard_map/ppermute | solution.py:546
  84.6 4.0 %collective-permute-done.13.refs_4_ = f32[192,128]{1,0:T(8,128)S(1)} collective-permute-done((f32[192,128]{1,0:T(8,128)S(1)}, f32[192,128]{1,0:T(8,128)S(1)}, u32[]{:S(2)}, u32[]{:S(2)}) %collective-permute-start.13) | collective-permute-done | bytes 98336 | tf_op jit(solution)/shard_map/ppermute | solution.py:546
  88.6 2.1 %collective-permute-done.14.refs_5_ = f32[192,128]{1,0:T(8,128)S(1)} collective-permute-done((f32[192,128]{1,0:T(8,128)S(1)}, f32[192,128]{1,0:T(8,128)S(1)}, u32[]{:S(2)}, u32[]{:S(2)}) %collective-permute-start.14) | collective-permute-done | bytes 98336 | tf_op jit(solution)/shard_map/ppermute | solution.py:546
  (41 shorter events, 11.4 us)
Async XLA Ops:
  4.0 55.1 %all-to-all-start = ((f32[8,192,128]{2,1,0:T(8,128)}), f32[8,192,128]{2,1,0:T(8,128)S(1)}, u32[]{:S(2)}, u32[]{:S(2)}) async-start(f32[8,192,128]{2,1,0:T(8,128)} %get-tuple-element.50), calls=%async_computation | async-start | bytes 1572864 | tf_op jit(solution)/shard_map/all_to_all | solution.py:543
  11.4 8.8 %collective-permute-start = (f32[136,128]{1,0:T(8,128)S(1)}, f32[136,128]{1,0:T(8,128)S(1)}, u32[]{:S(2)}, u32[]{:S(2)}) collective-permute-start(f32[136,128]{1,0:T(8,128)S(1)} %get-tuple-element.41), channel_id=1, source_target_pairs={{0,4},{4,0},{8,12},{12,8},{16,20},{20,16},{24,28},{28,24},{1,5},{5... | collective-permute-start | bytes 208904 | tf_op jit(solution)/shard_map/ppermute | solution.py:546
  13.4 13.4 %collective-permute-start.1 = (f32[136,128]{1,0:T(8,128)S(1)}, f32[136,128]{1,0:T(8,128)S(1)}, u32[]{:S(2)}, u32[]{:S(2)}) collective-permute-start(f32[136,128]{1,0:T(8,128)S(1)} %get-tuple-element.42), channel_id=1, source_target_pairs={{0,8},{4,12},{8,0},{12,4},{16,24},{20,28},{24,16},{28,20},{1,9},{5... | collective-permute-start | bytes 208904 | tf_op jit(solution)/shard_map/ppermute | solution.py:546
  14.9 16.7 %collective-permute-start.2 = (f32[136,128]{1,0:T(8,128)S(1)}, f32[136,128]{1,0:T(8,128)S(1)}, u32[]{:S(2)}, u32[]{:S(2)}) collective-permute-start(f32[136,128]{1,0:T(8,128)S(1)} %get-tuple-element.43), channel_id=1, source_target_pairs={{0,12},{4,8},{8,4},{12,0},{16,28},{20,24},{24,20},{28,16},{1,13},{... | collective-permute-start | bytes 208904 | tf_op jit(solution)/shard_map/ppermute | solution.py:546
  14.9 25.5 %collective-permute-start.3 = (f32[136,128]{1,0:T(8,128)S(1)}, f32[136,128]{1,0:T(8,128)S(1)}, u32[]{:S(2)}, u32[]{:S(2)}) collective-permute-start(f32[136,128]{1,0:T(8,128)S(1)} %get-tuple-element.44), channel_id=1, source_target_pairs={{0,16},{4,20},{8,24},{12,28},{16,0},{20,4},{24,8},{28,12},{1,17},{... | collective-permute-start | bytes 208904 | tf_op jit(solution)/shard_map/ppermute | solution.py:546
  17.8 24.5 %collective-permute-start.4 = (f32[136,128]{1,0:T(8,128)S(1)}, f32[136,128]{1,0:T(8,128)S(1)}, u32[]{:S(2)}, u32[]{:S(2)}) collective-permute-start(f32[136,128]{1,0:T(8,128)S(1)} %get-tuple-element.45), channel_id=1, source_target_pairs={{0,20},{4,16},{8,28},{12,24},{16,4},{20,0},{24,12},{28,8},{1,21},{... | collective-permute-start | bytes 208904 | tf_op jit(solution)/shard_map/ppermute | solution.py:546
  20.3 22.1 %collective-permute-start.5 = (f32[136,128]{1,0:T(8,128)S(1)}, f32[136,128]{1,0:T(8,128)S(1)}, u32[]{:S(2)}, u32[]{:S(2)}) collective-permute-start(f32[136,128]{1,0:T(8,128)S(1)} %get-tuple-element.46), channel_id=1, source_target_pairs={{0,24},{4,28},{8,16},{12,20},{16,8},{20,12},{24,0},{28,4},{1,25},{... | collective-permute-start | bytes 208904 | tf_op jit(solution)/shard_map/ppermute | solution.py:546
  26.8 15.5 %collective-permute-start.6 = (f32[136,128]{1,0:T(8,128)S(1)}, f32[136,128]{1,0:T(8,128)S(1)}, u32[]{:S(2)}, u32[]{:S(2)}) collective-permute-start(f32[136,128]{1,0:T(8,128)S(1)} %get-tuple-element.47), channel_id=1, source_target_pairs={{0,28},{4,24},{8,20},{12,16},{16,12},{20,8},{24,4},{28,0},{1,29},{... | collective-permute-start | bytes 208904 | tf_op jit(solution)/shard_map/ppermute | solution.py:546
  42.4 4.6 %collective-permute-start.9 = (f32[16,128]{1,0:T(8,128)S(1)}, f32[16,128]{1,0:T(8,128)S(1)}, u32[]{:S(2)}, u32[]{:S(2)}) collective-permute-start(f32[16,128]{1,0:T(8,128)S(1)} %pad_maximum_fusion.refs_0_), channel_id=1, source_target_pairs={{0,3},{1,0},{2,1},{3,2},{4,7},{5,4},{6,5},{7,6},{8,11},{9,8},{10,9... | collective-permute-start | bytes 24584 | tf_op jit(solution)/shard_map/ppermute | solution.py:564
  42.5 4.6 %collective-permute-start.8 = (f32[16,128]{1,0:T(8,128)S(1)}, f32[16,128]{1,0:T(8,128)S(1)}, u32[]{:S(2)}, u32[]{:S(2)}) collective-permute-start(f32[16,128]{1,0:T(8,128)S(1)} %pad_maximum_fusion.refs_0_), channel_id=1, source_target_pairs={{0,2},{1,3},{2,0},{3,1},{4,6},{5,7},{6,4},{7,5},{8,10},{9,11},{10,... | collective-permute-start | bytes 24584 | tf_op jit(solution)/shard_map/ppermute | solution.py:564
  52.8 10.3 %collective-permute-start.17 = (f32[128,128]{1,0:T(8,128)S(1)}, f32[128,128]{1,0:T(8,128)S(1)}, u32[]{:S(2)}, u32[]{:S(2)}) collective-permute-start(f32[128,128]{1,0:T(8,128)S(1)} %get-tuple-element.60), channel_id=1, source_target_pairs={{0,4},{4,0},{8,12},{12,8},{16,20},{20,16},{24,28},{28,24},{1,5},{5... | collective-permute-start | bytes 196616 | tf_op jit(solution)/shard_map/ppermute | solution.py:546
  53.8 9.7 %collective-permute-start.18 = (f32[128,128]{1,0:T(8,128)S(1)}, f32[128,128]{1,0:T(8,128)S(1)}, u32[]{:S(2)}, u32[]{:S(2)}) collective-permute-start(f32[128,128]{1,0:T(8,128)S(1)} %get-tuple-element.61), channel_id=1, source_target_pairs={{0,8},{4,12},{8,0},{12,4},{16,24},{20,28},{24,16},{28,20},{1,9},{5... | collective-permute-start | bytes 196616 | tf_op jit(solution)/shard_map/ppermute | solution.py:546
  56.0 11.2 %collective-permute-start.19 = (f32[128,128]{1,0:T(8,128)S(1)}, f32[128,128]{1,0:T(8,128)S(1)}, u32[]{:S(2)}, u32[]{:S(2)}) collective-permute-start(f32[128,128]{1,0:T(8,128)S(1)} %get-tuple-element.62), channel_id=1, source_target_pairs={{0,12},{4,8},{8,4},{12,0},{16,28},{20,24},{24,20},{28,16},{1,13},{... | collective-permute-start | bytes 196616 | tf_op jit(solution)/shard_map/ppermute | solution.py:546
  56.9 12.0 %collective-permute-start.20 = (f32[128,128]{1,0:T(8,128)S(1)}, f32[128,128]{1,0:T(8,128)S(1)}, u32[]{:S(2)}, u32[]{:S(2)}) collective-permute-start(f32[128,128]{1,0:T(8,128)S(1)} %get-tuple-element.63), channel_id=1, source_target_pairs={{0,16},{4,20},{8,24},{12,28},{16,0},{20,4},{24,8},{28,12},{1,17},{... | collective-permute-start | bytes 196616 | tf_op jit(solution)/shard_map/ppermute | solution.py:546
  62.9 17.4 %collective-permute-start.10 = (f32[192,128]{1,0:T(8,128)S(1)}, f32[192,128]{1,0:T(8,128)S(1)}, u32[]{:S(2)}, u32[]{:S(2)}) collective-permute-start(f32[192,128]{1,0:T(8,128)S(1)} %get-tuple-element.52), channel_id=1, source_target_pairs={{0,4},{4,0},{8,12},{12,8},{16,20},{20,16},{24,28},{28,24},{1,5},{5... | collective-permute-start | bytes 294920 | tf_op jit(solution)/shard_map/ppermute | solution.py:546
  63.1 19.2 %collective-permute-start.11 = (f32[192,128]{1,0:T(8,128)S(1)}, f32[192,128]{1,0:T(8,128)S(1)}, u32[]{:S(2)}, u32[]{:S(2)}) collective-permute-start(f32[192,128]{1,0:T(8,128)S(1)} %get-tuple-element.53), channel_id=1, source_target_pairs={{0,8},{4,12},{8,0},{12,4},{16,24},{20,28},{24,16},{28,20},{1,9},{5... | collective-permute-start | bytes 294920 | tf_op jit(solution)/shard_map/ppermute | solution.py:546
  63.6 8.8 %collective-permute-start.21 = (f32[128,128]{1,0:T(8,128)S(1)}, f32[128,128]{1,0:T(8,128)S(1)}, u32[]{:S(2)}, u32[]{:S(2)}) collective-permute-start(f32[128,128]{1,0:T(8,128)S(1)} %get-tuple-element.64), channel_id=1, source_target_pairs={{0,20},{4,16},{8,28},{12,24},{16,4},{20,0},{24,12},{28,8},{1,21},{... | collective-permute-start | bytes 196616 | tf_op jit(solution)/shard_map/ppermute | solution.py:546
  67.2 6.8 %collective-permute-start.22 = (f32[128,128]{1,0:T(8,128)S(1)}, f32[128,128]{1,0:T(8,128)S(1)}, u32[]{:S(2)}, u32[]{:S(2)}) collective-permute-start(f32[128,128]{1,0:T(8,128)S(1)} %get-tuple-element.65), channel_id=1, source_target_pairs={{0,24},{4,28},{8,16},{12,20},{16,8},{20,12},{24,0},{28,4},{1,25},{... | collective-permute-start | bytes 196616 | tf_op jit(solution)/shard_map/ppermute | solution.py:546
  68.8 8.7 %collective-permute-start.23 = (f32[128,128]{1,0:T(8,128)S(1)}, f32[128,128]{1,0:T(8,128)S(1)}, u32[]{:S(2)}, u32[]{:S(2)}) collective-permute-start(f32[128,128]{1,0:T(8,128)S(1)} %get-tuple-element.66), channel_id=1, source_target_pairs={{0,28},{4,24},{8,20},{12,16},{16,12},{20,8},{24,4},{28,0},{1,29},{... | collective-permute-start | bytes 196616 | tf_op jit(solution)/shard_map/ppermute | solution.py:546
  72.4 12.2 %collective-permute-start.12 = (f32[192,128]{1,0:T(8,128)S(1)}, f32[192,128]{1,0:T(8,128)S(1)}, u32[]{:S(2)}, u32[]{:S(2)}) collective-permute-start(f32[192,128]{1,0:T(8,128)S(1)} %get-tuple-element.54), channel_id=1, source_target_pairs={{0,12},{4,8},{8,4},{12,0},{16,28},{20,24},{24,20},{28,16},{1,13},{... | collective-permute-start | bytes 294920 | tf_op jit(solution)/shard_map/ppermute | solution.py:546
  74.0 14.6 %collective-permute-start.13 = (f32[192,128]{1,0:T(8,128)S(1)}, f32[192,128]{1,0:T(8,128)S(1)}, u32[]{:S(2)}, u32[]{:S(2)}) collective-permute-start(f32[192,128]{1,0:T(8,128)S(1)} %get-tuple-element.55), channel_id=1, source_target_pairs={{0,16},{4,20},{8,24},{12,28},{16,0},{20,4},{24,8},{28,12},{1,17},{... | collective-permute-start | bytes 294920 | tf_op jit(solution)/shard_map/ppermute | solution.py:546
  77.6 13.1 %collective-permute-start.14 = (f32[192,128]{1,0:T(8,128)S(1)}, f32[192,128]{1,0:T(8,128)S(1)}, u32[]{:S(2)}, u32[]{:S(2)}) collective-permute-start(f32[192,128]{1,0:T(8,128)S(1)} %get-tuple-element.56), channel_id=1, source_target_pairs={{0,20},{4,16},{8,28},{12,24},{16,4},{20,0},{24,12},{28,8},{1,21},{... | collective-permute-start | bytes 294920 | tf_op jit(solution)/shard_map/ppermute | solution.py:546
  80.4 10.3 %collective-permute-start.15 = (f32[192,128]{1,0:T(8,128)S(1)}, f32[192,128]{1,0:T(8,128)S(1)}, u32[]{:S(2)}, u32[]{:S(2)}) collective-permute-start(f32[192,128]{1,0:T(8,128)S(1)} %get-tuple-element.57), channel_id=1, source_target_pairs={{0,24},{4,28},{8,16},{12,20},{16,8},{20,12},{24,0},{28,4},{1,25},{... | collective-permute-start | bytes 294920 | tf_op jit(solution)/shard_map/ppermute | solution.py:546
  82.3 8.4 %collective-permute-start.16 = (f32[192,128]{1,0:T(8,128)S(1)}, f32[192,128]{1,0:T(8,128)S(1)}, u32[]{:S(2)}, u32[]{:S(2)}) collective-permute-start(f32[192,128]{1,0:T(8,128)S(1)} %get-tuple-element.58), channel_id=1, source_target_pairs={{0,28},{4,24},{8,20},{12,16},{16,12},{20,8},{24,4},{28,0},{1,29},{... | collective-permute-start | bytes 294920 | tf_op jit(solution)/shard_map/ppermute | solution.py:546
  (4 other events, 123.8 us)
